TPU v7x, 128 devices: a whole 4x4x4 slice. The times are simulated.
128 devices in a mesh: dp: 4 (over y), ctx: 32 (over x, z, core).
Axes of the slice: x: 4, y: 4, z: 4, core: 2. Of those that a mesh axis runs over, the one named last changes fastest.
Arguments:
- x_in: bfloat16 [4, 4096, 4096], P('dp', 'ctx'), may hold values from -6 to 6
- b_in: bfloat16 [4, 4096, 128], P('dp', 'ctx'), may hold values from -6 to 6
- c_in: bfloat16 [4, 4096, 128], P('dp', 'ctx'), may hold values from -6 to 6
- log_decay: int32 [4, 4096, 64], P('dp', 'ctx'), may hold values from 0 to 14000, as said below
- w_out: bfloat16 [4096, 2048], P(('dp', 'ctx')), may hold values from -0.09375 to 0.09375
- cotangent: bfloat16 [4, 4096, 2048], P('dp', 'ctx'), may hold values from -6 to 6
Outputs:
- out: bfloat16 [4, 4096, 2048], P('dp', 'ctx')
- grad_x: bfloat16 [4, 4096, 4096], P('dp', 'ctx')
- grad_b: bfloat16 [4, 4096, 128], P('dp', 'ctx')
- gradient_c_input: bfloat16 [4, 4096, 128], P('dp', 'ctx')
Inputs may be any that keep to these rules, and one draw needn't show every extreme that they name: log_decay holds each head's per-token log-decay as a whole number.
All inputs are finite; a program needn't handle non-finite values.
Results may differ from a plain program's by a relative error of at most 0.01.
Values may be sent and summed in bfloat16 or wider, within the bound.
A program may use at most 320 MiB of HBM per device.

v0:
```python
import jax
import jax.numpy as jnp
from jax import lax
from jax.sharding import PartitionSpec as P

decay_unit = 5e-05


def causal_decay(local_group):
    cum = local_group.T
    rows = cum.shape[1]
    diff = (cum[:, :, None] - cum[:, None, :]).astype(jnp.float32)
    lower = lax.broadcasted_iota(jnp.int32, (rows, rows), 0) >= lax.broadcasted_iota(
        jnp.int32, (rows, rows), 1
    )
    return jnp.where(lower[None], jnp.exp(-decay_unit * diff), jnp.float32(0.0))


def forward_inside_group(x_bf, local, scores, scale, group, width):
    rows, inner = x_bf.shape
    heads = local.shape[1]
    count = heads // group
    x_groups = x_bf.reshape(rows, count, group, width).transpose(1, 0, 2, 3)
    l_groups = local.reshape(rows, count, group).transpose(1, 0, 2)

    def forward_one_group(carry, item):
        x_part, l_part = item
        mix = (scale * scores[None] * causal_decay(l_part)).astype(jnp.bfloat16)
        part = jnp.einsum("gtr,rgp->tgp", mix, x_part, preferred_element_type=jnp.float32)
        return (carry, (mix, part))

    _, (mixes, parts) = lax.scan(
        forward_one_group, jnp.zeros((), jnp.float32), (x_groups, l_groups)
    )
    return (mixes, parts.transpose(1, 0, 2, 3).reshape(rows, inner))


def backward_intra(mixes, x_bf, back_bf, local, scale, group, width):
    rows, inner = x_bf.shape
    heads = local.shape[1]
    count = heads // group
    x_groups = x_bf.reshape(rows, count, group, width).transpose(1, 0, 2, 3)
    d_groups = back_bf.reshape(rows, count, group, width).transpose(1, 0, 2, 3)
    l_groups = local.reshape(rows, count, group).transpose(1, 0, 2)

    def backward_one_group(total, item):
        mix, x_part, d_part, l_part = item
        flowed = jnp.einsum("gtr,tgp->rgp", mix, d_part, preferred_element_type=jnp.float32)
        inner_prod = jnp.einsum("tgp,rgp->gtr", d_part, x_part, preferred_element_type=jnp.float32)
        total = total + jnp.sum(scale * causal_decay(l_part) * inner_prod, axis=0)
        return (total, flowed)

    kernel, flows = lax.scan(
        backward_one_group,
        jnp.zeros((rows, rows), jnp.float32),
        (mixes, x_groups, d_groups, l_groups),
    )
    return (kernel, flows.transpose(1, 0, 2, 3).reshape(rows, inner))


def body(x_in, b_in, c_in, log_decay, w_out, cotangent):
    x_bf = x_in[0]
    b_blk = b_in[0]
    c_blk = c_in[0]
    steps = log_decay[0]
    grad_out = cotangent[0]
    rows, inner = x_bf.shape
    heads = steps.shape[1]
    width = inner // heads
    length = rows * lax.axis_size("ctx")
    scale = (b_blk.shape[1] * length) ** (-0.5)
    group = 8
    local = jnp.cumsum(steps, axis=0)
    totals = local[-1]
    fall_wide = jnp.repeat(jnp.exp(-decay_unit * local.astype(jnp.float32)), width, axis=1)
    tail_wide = jnp.repeat(
        jnp.exp(-decay_unit * (totals[None, :] - local).astype(jnp.float32)), width, axis=1
    )
    scores = jnp.dot(c_blk, b_blk.T, preferred_element_type=jnp.float32)
    mixes, y_intra = forward_inside_group(x_bf, local, scores, scale, group, width)
    shifted = (x_bf * tail_wide).astype(jnp.bfloat16)
    term = jnp.dot(b_blk.T, shifted, preferred_element_type=jnp.float32)
    mine = lax.axis_index("ctx")
    all_totals = lax.all_gather(totals[None, :], "ctx", axis=0, tiled=True)
    before_sum = jnp.cumsum(all_totals, axis=0) - all_totals
    mine_before = lax.dynamic_slice_in_dim(before_sum, mine, 1, 0)
    mine_total = lax.dynamic_slice_in_dim(all_totals, mine, 1, 0)

    def weighted_add(carry, piece, later):
        count = piece.shape[0]
        index_set = jnp.arange(count, dtype=jnp.int32)
        if later:
            span = before_sum - mine_before - mine_total
            live = index_set > mine
        else:
            span = mine_before - before_sum - all_totals
            live = index_set < mine
        span = jnp.maximum(span, 0).astype(jnp.float32)
        weight = jnp.where(live[:, None], jnp.exp(-decay_unit * span), jnp.float32(0.0))
        weight_wide = jnp.repeat(weight, width, axis=1)
        return carry + jnp.einsum("ksi,ki->si", piece, weight_wide, precision=lax.Precision.HIGHEST)

    before = weighted_add(
        jnp.zeros_like(term), lax.all_gather(term[None], "ctx", axis=0, tiled=True), False
    )
    before_bf = before.astype(jnp.bfloat16)
    mixed = (
        y_intra + scale * fall_wide * jnp.dot(c_blk, before_bf, preferred_element_type=jnp.float32)
    ).astype(jnp.bfloat16)
    whole_proj = lax.all_gather(w_out, ("dp", "ctx"), axis=0, tiled=True)
    out = jnp.dot(mixed, whole_proj, preferred_element_type=jnp.float32).astype(jnp.bfloat16)
    back_bf = lax.dot_general(
        grad_out, whole_proj, (((1,), (1,)), ((), ())), preferred_element_type=jnp.float32
    ).astype(jnp.bfloat16)
    dshift = (back_bf * fall_wide).astype(jnp.bfloat16)
    adjoint_term = jnp.dot(c_blk.T, dshift, preferred_element_type=jnp.float32)
    after = weighted_add(
        jnp.zeros_like(adjoint_term),
        lax.all_gather(adjoint_term[None].astype(jnp.bfloat16), "ctx", axis=0, tiled=True).astype(
            jnp.float32
        ),
        True,
    )
    after_bf = after.astype(jnp.bfloat16)
    kernel, dx_intra = backward_intra(mixes, x_bf, back_bf, local, scale, group, width)
    kernel_bf = kernel.astype(jnp.bfloat16)
    grad_x = (
        dx_intra + scale * tail_wide * jnp.dot(b_blk, after_bf, preferred_element_type=jnp.float32)
    ).astype(jnp.bfloat16)
    grad_b = (
        jnp.dot(kernel_bf.T, c_blk, preferred_element_type=jnp.float32)
        + scale * jnp.dot(shifted, after_bf.T, preferred_element_type=jnp.float32)
    ).astype(jnp.bfloat16)
    gradient_c_input = (
        jnp.dot(kernel_bf, b_blk, preferred_element_type=jnp.float32)
        + scale * jnp.dot(dshift, before_bf.T, preferred_element_type=jnp.float32)
    ).astype(jnp.bfloat16)
    return (out[None], grad_x[None], grad_b[None], gradient_c_input[None])


def solution(mesh):
    in_specs = (
        P("dp", "ctx", None),
        P("dp", "ctx", None),
        P("dp", "ctx", None),
        P("dp", "ctx", None),
        P(("dp", "ctx"), None),
        P("dp", "ctx", None),
    )
    out_specs = (
        P("dp", "ctx", None),
        P("dp", "ctx", None),
        P("dp", "ctx", None),
        P("dp", "ctx", None),
    )
    return jax.shard_map(body, mesh=mesh, in_specs=in_specs, out_specs=out_specs, check_vma=False)
```

profile of v0, /device:TPU:1, one launch (start us, length us, event | category | flops | bytes accessed | tf_op | source)
XLA Modules:
  0.0 575.8 jit_solution(17110521173736781467)
XLA Ops:
  9.3 1.9 copy.35
  11.2 83.5 %all-gather.7.cloned.1.call-done = bf16[4096,2048]{1,0:T(8,128)(2,1)} async-done(((bf16[32,2048]{1,0:T(8,128)(2,1)}), bf16[4096,2048]{1,0:T(8,128)(2,1)}) %all-gather.7.cloned.1.call-update) | async-done | bytes 16777232 | tf_op jit(solution)/shard_map/all_gather | solution.py:110
  94.8 12.6 %convolution_convert_fusion = bf16[128,4096]{1,0:T(8,128)(2,1)} fusion(bf16[4096,2048]{1,0:T(8,128)(2,1)} %all-gather.7.cloned.1.call-done, bf16[1,128,2048]{2,1,0:T(8,128)(2,1)S(1)} %copy-done), kind=kOutput, calls=%fused_computation.43 | convolution fusion | flops 2148007936 | bytes 18350080 | tf_op jit(solution)/shard_map/dot_general | solution.py:112
  107.4 2.7 fusion.31
  110.2 1.6 copy.30
  112.2 1.8 convolution_bitcast_fusion.4
  114.0 1.9 fusion.34
  116.0 21.5 %all-gather.2 = s32[32,1,64]{2,1,0:T(1,128)S(1)} all-gather(s32[1,1,64]{2,1,0:T(1,128)S(1)} %get-tuple-element.140), channel_id=1, replica_groups=mesh['dp'=4,'ctx'=32] {'ctx'}, dimensions={0}, use_global_device_ids=true | all-gather | bytes 8448 | tf_op jit(solution)/shard_map/all_gather | solution.py:84
  138.0 1.7 broadcast.94.clone
  139.7 16.4 %while.25 = (s32[]{:T(128)}, bf16[8,8,128,128]{3,2,1,0:T(8,128)(2,1)}, f32[8,128,8,64]{1,3,2,0:T(8,128)}, f32[128,128]{1,0:T(8,128)S(1)}, s32[8,128,8]{1,2,0:T(8...) while((s32[]{:T(128)}, bf16[8,8,128,128]{3,2,1,0:T(8,128)(2,1)}, f32[8,128,8,64]{1,3,2,0:T(8,128)}, ...), condition=%wide.region_2.3_spmd, body=%wide.region_1.2_spmd.sunk | while | flops 18382848 | bytes 992349 | solution.py:32
  139.7 1.1 fusion.84
  141.7 1.1 fusion.84
  143.8 1.1 fusion.84
  145.9 1.1 fusion.84
  147.9 1.1 fusion.84
  150.0 1.1 fusion.84
  152.0 1.1 fusion.84
  154.0 1.1 fusion.84
  156.0 1.3 copy.34
  157.3 1.6 broadcast.94
  159.0 26.1 %while.26 = (s32[]{:T(128)}, f32[128,128]{1,0:T(8,128)S(1)}, f32[8,128,8,64]{1,3,2,0:T(8,128)}, s32[8,128,8]{1,2,0:T(8,128)S(1)}, bf16[8,128,8,64]{1,3,2,0:T(8,1...) while((s32[]{:T(128)}, f32[128,128]{1,0:T(8,128)S(1)}, ...), condition=%wide.region_6.7_spmd.clone, body=%wide.region_4.6_spmd.clone.sunk | while | flops 34504704 | bytes 1231475 | solution.py:53
  159.0 1.3 fusion.89
  160.3 2.0 fusion.90
  162.2 1.3 fusion.89
  163.5 2.0 fusion.90
  165.5 1.2 fusion.89
  166.8 1.9 fusion.90
  168.7 1.2 fusion.89
  170.0 1.9 fusion.90
  172.0 1.2 fusion.89
  173.2 1.9 fusion.90
  175.2 1.2 fusion.89
  176.5 1.9 fusion.90
  178.4 1.2 fusion.89
  179.7 2.1 fusion.90
  181.8 1.3 fusion.89
  183.1 2.0 fusion.90
  185.4 49.2 %all-gather.11.cloned.1.call-done = bf16[4096,4096]{0,1:T(8,128)(2,1)} async-done(((bf16[128,4096]{0,1:T(8,128)(2,1)}), bf16[4096,4096]{0,1:T(8,128)(2,1)}) %all-gather.11.cloned.1.call-update) | async-done | bytes 33554448 | tf_op jit(solution)/shard_map/all_gather | solution.py:119
  234.5 23.8 %copy.46 = bf16[512,8,32,128]{3,2,1,0:T(8,128)(2,1)} copy(bf16[512,8,32,128]{3,1,2,0:T(8,128)(2,1)} %bitcast.164) | data formatting | bytes 67108864
  258.5 29.8 %fusion.64 = f32[4096,1,128]{2,1,0:T(1,128)S(1)} fusion(f32[32,4096,1]{0,2,1:T(1,128)S(1)} %bitcast.179, bf16[32,128,4096]{1,0,2:T(8,128)(2,1)} %bitcast.165), kind=kOutput, calls=%fused_computation.95 | convolution fusion | flops 201326592 | bytes 36175872 | tf_op jit(solution)/shard_map/ksi,ki->si/dot_general | solution.py:101
  288.4 1.5 fusion.32
  289.9 2.3 copy.36
  292.1 2.3 fusion.40
  294.4 159.6 %all-gather.9.cloned.1.call-done = f32[4096,4096]{0,1:T(8,128)} async-done(((f32[128,4096]{0,1:T(8,128)}), f32[4096,4096]{0,1:T(8,128)}) %all-gather.9.cloned.1.call-update) | async-done | bytes 67108880 | tf_op jit(solution)/shard_map/all_gather | solution.py:104
  454.0 44.1 %copy.45 = f32[512,8,32,128]{3,2,1,0:T(8,128)} copy(f32[512,8,32,128]{3,1,2,0:T(8,128)} %bitcast.60) | data formatting | bytes 134217728
  498.3 58.8 %fusion.63 = f32[4096,1,128]{2,1,0:T(1,128)S(1)} fusion(f32[32,4096,1]{0,2,1:T(1,128)S(1)} %bitcast.170, f32[32,128,4096]{1,0,2:T(8,128)} %bitcast.62), kind=kOutput, calls=%fused_computation.94 | convolution fusion | flops 201326592 | bytes 69730304 | tf_op jit(solution)/shard_map/ksi,ki->si/dot_general | solution.py:101
  557.2 1.1 fusion.39
  558.3 11.0 %fusion.33 = bf16[1,128,2048]{2,1,0:T(8,128)(2,1)} fusion(bf16[4096,2048]{1,0:T(8,128)(2,1)} %all-gather.7.cloned.1.call-done, f32[128,4096]{0,1:T(8,128)} %bitcast.176, f32[128,4096]{0,1:T(8,128)} %bitcast.169, f32[4096,128]{1,0:T(8,128)S(1)} %bitcast.167, bf16[1,128,128]{2,1,0:T(8,128)(2,1)S(1)} %copy-done.10), kind=kOutput, calls=%fused_computation.52 | convolution fusion | flops 2284584960 | bytes 23625728 | tf_op jit(solution)/shard_map/dot_general | solution.py:111
  (108 shorter events, 11.5 us)
Async XLA Ops:
  7.2 87.6 %copy-start = (bf16[1,128,2048]{2,1,0:T(8,128)(2,1)S(1)}, bf16[1,128,2048]{2,1,0:T(8,128)(2,1)}, u32[]{:S(2)}) copy-start(bf16[1,128,2048]{2,1,0:T(8,128)(2,1)} %param.15) | copy-start | bytes 1572868
  7.2 87.6 %all-gather.7.cloned.1.call-start = ((), (), s32[]{:S(2)}) async-start(), calls=%async_computation | async-start | bytes 16908288 | tf_op jit(solution)/shard_map/all_gather | solution.py:110
  7.9 226.6 %all-gather.11.cloned.1.call-start = ((), (), s32[]{:S(2)}) async-start(), calls=%async_computation.2 | async-start | bytes 34603008 | tf_op jit(solution)/shard_map/all_gather | solution.py:119
  9.3 2.0 copy-start.2
  11.2 96.1 %copy-start.10 = (bf16[1,128,128]{2,1,0:T(8,128)(2,1)S(1)}, bf16[1,128,128]{2,1,0:T(8,128)(2,1)}, u32[]{:S(2)}) copy-start(bf16[1,128,128]{2,1,0:T(8,128)(2,1)} %param.12) | copy-start | bytes 98308
  94.8 12.6 %copy-start.3 = (f32[128,4096]{1,0:T(8,128)S(1)}, f32[128,4096]{1,0:T(8,128)}, u32[]{:S(2)}) copy-start(f32[128,4096]{1,0:T(8,128)} %copy.35) | copy-start | bytes 6291460
  110.1 343.9 %all-gather.9.cloned.1.call-start = ((), (), s32[]{:S(2)}) async-start(), calls=%async_computation.1 | async-start | bytes 69206016 | tf_op jit(solution)/shard_map/all_gather | solution.py:104
  110.2 2.0 copy-start.9
  139.7 16.4 %copy-start.5 = (bf16[128,4096]{1,0:T(8,128)(2,1)S(1)}, bf16[128,4096]{1,0:T(8,128)(2,1)}, u32[]{:S(2)}) copy-start(bf16[128,4096]{1,0:T(8,128)(2,1)} %convolution_convert_fusion) | copy-start | bytes 3145732
  258.5 29.8 %copy-start.7 = (f32[128,4096]{0,1:T(8,128)S(1)}, f32[128,4096]{0,1:T(8,128)}, u32[]{:S(2)}) copy-start(f32[128,4096]{0,1:T(8,128)} %get-tuple-element.142) | copy-start | bytes 6291460
  258.5 29.8 %copy-start.8 = (f32[8,128,8,64]{1,3,2,0:T(8,128)S(1)}, f32[8,128,8,64]{1,3,2,0:T(8,128)}, u32[]{:S(2)}) copy-start(f32[8,128,8,64]{1,3,2,0:T(8,128)} %get-tuple-element.77) | copy-start | bytes 6291460
  498.3 58.9 %copy-start.4 = (f32[128,4096]{1,0:T(8,128)S(1)}, f32[128,4096]{1,0:T(8,128)}, u32[]{:S(2)}) copy-start(f32[128,4096]{1,0:T(8,128)} %copy.35) | copy-start | bytes 6291460
  498.3 58.9 %copy-start.6 = (bf16[128,4096]{1,0:T(8,128)(2,1)S(1)}, bf16[128,4096]{1,0:T(8,128)(2,1)}, u32[]{:S(2)}) copy-start(bf16[128,4096]{1,0:T(8,128)(2,1)} %convolution_convert_fusion) | copy-start | bytes 3145732
  558.3 11.0 %copy-start.1 = (bf16[1,128,2048]{2,1,0:T(8,128)(2,1)S(1)}, bf16[1,128,2048]{2,1,0:T(8,128)(2,1)}, u32[]{:S(2)}) copy-start(bf16[1,128,2048]{2,1,0:T(8,128)(2,1)} %param.15) | copy-start | bytes 1572868
Sparse Core Ops, SparseCore 0:
  11.1 83.5 all-gather.6
  110.2 124.2 all-gather.10
  236.7 217.2 all-gather.8
where the time goes:
time: 576 us
  waiting for transfers between devices  293 us (51%)
  matrix products  156 us (27%)
  local copies, waits for them, and re-layouts  80.1 us (14%)
  blocking collectives  21.5 us (4%)
  between operations  14 us (2%)
  other arithmetic  10.4 us (2%)
    all_gather x1, waiting for transfers between devices, body(): lax.all_gather(term[None], 'ctx', axis=0, tiled=True)  160 us
    dot_general x2, matrix products, weighted_add(): jnp.einsum('ksi,ki->si', piece, weight_wide, precision=lax.Precision.HIGH...  88.7 us
    all_gather x1, waiting for transfers between devices, body(): whole_proj = lax.all_gather(w_out, ('dp', 'ctx'), axis=0, tiled=True)  83.5 us
    unnamed x28, local copies, waits for them, and re-layouts  72.1 us
    all_gather x1, waiting for transfers between devices, body(): lax.all_gather(adjoint_term[None].astype(jnp.bfloat16), 'ctx', axis=0, ti...  49.2 us
    all_gather x1, blocking collectives, body(): all_totals = lax.all_gather(totals[None, :], 'ctx', axis=0, tiled=True)  21.5 us
    dot_general x8, matrix products, backward_one_group(): jnp.einsum('gtr,tgp->rgp', mix, d_part, preferred_element_type=jnp.float32)  15.7 us
    dot_general x1, matrix products, body(): lax.dot_general(grad_out, whole_proj, (((1,), (1,)), ((), ())), preferred...  12.6 us
  transfers between devices with their start and end apart: 3, of which 3 were waited for; matrix products, arithmetic and copies ran while one was open for 20% of the time, Pallas kernels for 0%

commit v1 on v0

--- a/solution.py
+++ b/solution.py
@@ -101,7 +101,11 @@
         return carry + jnp.einsum("ksi,ki->si", piece, weight_wide, precision=lax.Precision.HIGHEST)
 
     before = weighted_add(
-        jnp.zeros_like(term), lax.all_gather(term[None], "ctx", axis=0, tiled=True), False
+        jnp.zeros_like(term),
+        jnp.concatenate(
+            lax.all_to_all(jnp.stack([term[None]] * lax.axis_size("ctx")), "ctx", 0, 0), axis=0
+        ),
+        False,
     )
     before_bf = before.astype(jnp.bfloat16)
     mixed = (

time: 576 us -> 1420 us (2.47)
  waiting for transfers between devices: 293 us -> 750 us
  blocking collectives: 21.5 us -> 433 us
  matrix products: 156 us -> 107 us
  other arithmetic: 10.4 us -> 33.9 us
    all_gather x1, waiting for transfers between devices: 83.5 us -> 749 us  [body(): whole_proj = lax.all_gather(w_out, ('dp', 'ctx'), axis=0, tiled=True)]
    all_gather x1, blocking collectives: 21.5 us -> 433 us  [body(): all_totals = lax.all_gather(totals[None, :], 'ctx', axis=0, tiled=True)]
    all_gather x1 -> x0, waiting for transfers between devices: 160 us -> none  [body(): lax.all_gather(term[None], 'ctx', axis=0, tiled=True)]
    dot_general x2 -> x1, matrix products: 88.7 us -> 29.8 us  [weighted_add(): jnp.einsum('ksi,ki->si', piece, weight_wide, precision=lax.Precision.HIGH...]
    all_gather x1, waiting for transfers between devices: 49.2 us -> 0.01 us  [body(): lax.all_gather(adjoint_term[None].astype(jnp.bfloat16), 'ctx', axis=0, ti...]
    unnamed x28 -> x23, local copies, waits for them, and re-layouts: 72.1 us -> 28.5 us
    another operation x2 -> x3, local copies, waits for them, and re-layouts: 3.28 us -> 25.9 us  [the longest x1 22.7 us: body(): jnp.stack([term[None]] * lax.axis_size('ctx'))]
    unnamed x1 -> x2, other arithmetic: 0.01 us -> 22.3 us
  transfers between devices with their start and end apart: 3 -> 3, of which waited for: 3 -> 1; matrix products, arithmetic and copies ran while one was open for 20% -> 11% of each run, Pallas kernels for 0% -> 0%
where the time goes in v1:
time: 1420 us
  waiting for transfers between devices  750 us (53%)
  blocking collectives  433 us (30%)
  matrix products  107 us (8%)
  local copies, waits for them, and re-layouts  69.6 us (5%)
  other arithmetic  33.9 us (2%)
    all_gather x1, waiting for transfers between devices, body(): whole_proj = lax.all_gather(w_out, ('dp', 'ctx'), axis=0, tiled=True)  749 us
    all_gather x1, blocking collectives, body(): all_totals = lax.all_gather(totals[None, :], 'ctx', axis=0, tiled=True)  433 us
    dot_general x1, matrix products, weighted_add(): jnp.einsum('ksi,ki->si', piece, weight_wide, precision=lax.Precision.HIGH...  29.8 us
    unnamed x23, local copies, waits for them, and re-layouts  28.5 us
  transfers between devices with their start and end apart: 3, of which 1 were waited for; matrix products, arithmetic and copies ran while one was open for 11% of the time, Pallas kernels for 0%

profile of v1, /device:TPU:1, one launch (start us, length us, event | category | flops | bytes accessed | tf_op | source)
XLA Modules:
  0.0 1417.0 jit_solution(4171267866970410772)
XLA Ops:
  9.1 1.6 copy.32
  11.1 1.8 convolution_bitcast_fusion.4
  12.8 3.0 copy.36
  15.8 22.7 %stack.3 = f32[32,1,128,4096]{3,2,1,0:T(8,128)} broadcast(f32[128,4096]{1,0:T(8,128)} %copy.36), dimensions={2,3} | broadcast | bytes 69206016 | tf_op jit(solution)/shard_map/stack | solution.py:106
  38.5 9.5 all-to-all-start
  48.1 1.5 broadcast_in_dim.92
  49.6 2.0 copy.38
  51.6 749.4 %all-gather.5.cloned.1.call-done = bf16[4096,2048]{1,0:T(8,128)(2,1)} async-done(((bf16[32,2048]{1,0:T(8,128)(2,1)}), bf16[4096,2048]{1,0:T(8,128)(2,1)}) %all-gather.5.cloned.1.call-update) | async-done | bytes 16777232 | tf_op jit(solution)/shard_map/all_gather | solution.py:114
  801.0 12.4 convolution_convert_fusion
  813.4 2.7 fusion.32
  816.2 3.2 fusion.35
  819.4 432.7 %all-gather.1 = s32[32,1,64]{2,1,0:T(1,128)S(1)} all-gather(s32[1,1,64]{2,1,0:T(1,128)S(1)} %get-tuple-element.137), channel_id=1, replica_groups=mesh['dp'=4,'ctx'=32] {'ctx'}, dimensions={0}, use_global_device_ids=true | all-gather | bytes 8448 | tf_op jit(solution)/shard_map/all_gather | solution.py:84
  1252.2 1.3 broadcast_in_dim.95
  1253.6 1.6 reshape.117
  1255.4 1.6 broadcast.96.clone
  1257.0 23.5 %while.25 = (s32[]{:T(128)}, bf16[8,8,128,128]{3,2,1,0:T(8,128)(2,1)}, f32[8,128,8,64]{1,3,2,0:T(8,128)}, f32[128,128]{1,0:T(8,128)S(1)}, s32[8,128,8]{1,2,0:T(8...) while((s32[]{:T(128)}, bf16[8,8,128,128]{3,2,1,0:T(8,128)(2,1)}, f32[8,128,8,64]{1,3,2,0:T(8,128)}, ...), condition=%wide.region_2.3_spmd, body=%wide.region_1.2_spmd.sunk | while | flops 18382848 | bytes 992849 | solution.py:32
  1257.0 2.0 fusion.84
  1260.0 2.0 fusion.84
  1262.9 2.0 fusion.84
  1265.9 2.0 fusion.84
  1268.8 2.0 fusion.84
  1271.7 2.0 fusion.84
  1274.7 2.0 fusion.84
  1277.6 2.0 fusion.84
  1280.5 2.3 copy.37
  1282.8 1.6 broadcast.96
  1284.4 26.5 %while.26 = (s32[]{:T(128)}, f32[128,128]{1,0:T(8,128)S(1)}, f32[8,128,8,64]{1,3,2,0:T(8,128)}, s32[8,128,8]{1,2,0:T(8,128)S(1)}, bf16[8,128,8,64]{1,3,2,0:T(8,1...) while((s32[]{:T(128)}, f32[128,128]{1,0:T(8,128)S(1)}, ...), condition=%wide.region_6.7_spmd.clone, body=%wide.region_4.6_spmd.clone.sunk | while | flops 34504704 | bytes 1231467 | solution.py:53
  1284.4 1.3 fusion.89
  1285.8 1.9 fusion.90
  1289.1 1.9 fusion.90
  1291.1 1.3 fusion.89
  1292.4 1.9 fusion.90
  1295.7 1.9 fusion.90
  1299.0 1.9 fusion.90
  1301.0 1.3 fusion.89
  1302.3 1.9 fusion.90
  1305.6 2.0 fusion.90
  1309.0 1.9 fusion.90
  1311.2 22.2 %fusion.25 = bf16[4096,128]{0,1:T(8,128)(2,1)} fusion(f32[32,1,128,4096]{3,2,1,0:T(8,128)} %all-to-all-done, f32[4096,32]{0,1:T(8,128)S(1)} %bitcast.176), kind=kLoop, calls=%fused_computation.37 | loop fusion | flops 33030144 | bytes 68681728
  1333.5 2.3 copy.46
  1335.7 2.6 fusion.40
  1338.3 11.2 fusion.34
  1349.5 23.0 %copy.52 = bf16[512,8,32,128]{3,2,1,0:T(8,128)(2,1)} copy(bf16[512,8,32,128]{3,1,2,0:T(8,128)(2,1)} %bitcast.164) | data formatting | bytes 67108864
  1372.7 29.8 %fusion.64 = f32[4096,1,128]{2,1,0:T(1,128)S(1)} fusion(f32[32,4096,1]{0,2,1:T(1,128)S(1)} %bitcast.177, bf16[32,128,4096]{1,0,2:T(8,128)(2,1)} %bitcast.165), kind=kOutput, calls=%fused_computation.96 | convolution fusion | flops 201326592 | bytes 36175872 | tf_op jit(solution)/shard_map/ksi,ki->si/dot_general | solution.py:101
  1402.6 1.3 copy-done.4
  1403.9 1.5 fusion.33
  1405.4 2.4 copy.39
  1407.8 2.3 fusion.41
  (105 shorter events, 17.6 us)
Async XLA Ops:
  7.2 793.8 %copy-start = (bf16[1,128,2048]{2,1,0:T(8,128)(2,1)S(1)}, bf16[1,128,2048]{2,1,0:T(8,128)(2,1)}, u32[]{:S(2)}) copy-start(bf16[1,128,2048]{2,1,0:T(8,128)(2,1)} %param.15) | copy-start | bytes 1572868
  7.2 793.8 %all-gather.5.cloned.1.call-start = ((), (), s32[]{:S(2)}) async-start(), calls=%async_computation.1 | async-start | bytes 16908288 | tf_op jit(solution)/shard_map/all_gather | solution.py:114
  9.1 2.0 copy-start.8
  10.7 2.1 copy-start.2
  38.5 1272.7 %all-to-all-start = ((f32[32,1,128,4096]{3,2,1,0:T(8,128)}), f32[32,1,128,4096]{3,2,1,0:T(8,128)}, u32[]{:S(2)}, u32[]{:S(2)}) async-start(f32[32,1,128,4096]{3,2,1,0:T(8,128)} %stack.3), calls=%async_computation | async-start | bytes 134217728 | tf_op jit(solution)/shard_map/all_to_all | solution.py:106
  48.0 1301.6 %all-gather.7.cloned.1.call-start = ((), (), s32[]{:S(2)}) async-start(), calls=%async_computation.2 | async-start | bytes 34603008 | tf_op jit(solution)/shard_map/all_gather | solution.py:123
  51.6 761.8 %copy-start.7 = (bf16[1,128,128]{2,1,0:T(8,128)(2,1)S(1)}, bf16[1,128,128]{2,1,0:T(8,128)(2,1)}, u32[]{:S(2)}) copy-start(bf16[1,128,128]{2,1,0:T(8,128)(2,1)} %param.12) | copy-start | bytes 98308
  1372.7 31.2 %copy-start.3 = (f32[128,4096]{0,1:T(8,128)S(1)}, f32[128,4096]{0,1:T(8,128)}, u32[]{:S(2)}) copy-start(f32[128,4096]{0,1:T(8,128)} %get-tuple-element.142) | copy-start | bytes 6291460
  1372.7 31.2 %copy-start.6 = (f32[8,128,8,64]{1,3,2,0:T(8,128)S(1)}, f32[8,128,8,64]{1,3,2,0:T(8,128)}, u32[]{:S(2)}) copy-start(f32[8,128,8,64]{1,3,2,0:T(8,128)} %get-tuple-element.77) | copy-start | bytes 6291460
  1402.6 1.3 copy-start.4
  1405.4 2.4 copy-start.5
  1405.4 4.7 copy-start.1
Sparse Core Ops, SparseCore 0:
  11.1 789.8 all-gather.4
  816.2 272.0 all-gather.6
